TPU v7x, 256 devices: a whole 4x4x8 slice. The times are simulated.
256 devices in a mesh: gx: 16 (over z, core), gy: 8 (over y_lo, x), col: 2 (over y_hi).
Axes of the slice: x: 4, y: 4 (y_hi: 2, y_lo: 2; y = y_hi * 2 + y_lo), z: 8, core: 2. Of those that a mesh axis runs over, the one named last changes fastest.
Arguments:
- field: bfloat16 [64, 32, 128, 128], P(None, 'gx', 'gy'), may hold values from -6 to 6
- first_weight: bfloat16 [64, 64, 3, 3, 3], P('col'), may hold values from -0.21875 to 0.21875
- second_weight: bfloat16 [64, 64, 3, 3, 3], P('col'), may hold values from -0.21875 to 0.21875
- up_weight: bfloat16 [32, 64, 4, 4, 4], P('col'), may hold values from -0.375 to 0.375
Outputs:
- upsampled: bfloat16 [32, 64, 256, 256], P('col', 'gx', 'gy')
All inputs are finite; a program needn't handle non-finite values.
Results may differ from a plain program's by a relative error of at most 0.0059.
Values may be sent and summed in bfloat16 or wider, within the bound.
A program may use at most 64 MiB of HBM per device.

v0:
```python
import functools

import jax
import jax.numpy as jnp
from jax import lax
from jax.experimental import pallas as pl
from jax.experimental.pallas import tpu as pltpu
from jax.sharding import PartitionSpec as P

C = 64
NZ = 128
ROWS = 16
DEPTH = 3
MESH = pl.DeviceIdType.MESH
MIDDLE = tuple(range(1, 15))
BORDER = (-2, -1, 0, 15, 16, 17)
MIDDLE_2 = tuple(range(2, 14))
BORDER_2 = (-1, 0, 1, 14, 15, 16)
MIDDLE_3 = tuple(range(3, 13))
BORDER_3 = (0, 1, 2, 13, 14, 15)
COPIES = 28


def pairs(items):
    return [items[i : i + 2] for i in range(0, len(items), 2)]


def block(first, count):
    return pl.ds(first * C, count * C)


def taps_matmul(weight, cells, source, span):
    columns = [
        jnp.concatenate([source[layer, block(row, span), :] for layer in layers], axis=0) for layers, row in cells
    ]
    return jnp.dot(weight, jnp.concatenate(columns, axis=1), preferred_element_type=jnp.float32)


def convolve(weight_ref, source, source_at, target, target_at, layer, rows):
    weight = weight_ref[...]
    for pair in pairs(rows):
        cells = [([layer + k + source_at for k in (-1, 0, 1)], row - 1 + source_at) for row in pair]
        taps = taps_matmul(weight, cells, source, 3)
        for i, row in enumerate(pair):
            for half in range(2):
                tap = taps[half * 96 : half * 96 + 96, i * NZ : (i + 1) * NZ]
                value = pltpu.roll(tap[:32], 1, 1) + tap[32:64] + pltpu.roll(tap[64:], NZ - 1, 1)
                start = (row + target_at) * C + half * 32
                target[layer + target_at, start : start + 32, :] = jnp.maximum(value, 0.0).astype(jnp.bfloat16)


def refine(core, weight_ref, source, fine, layer, rows):
    for along_x in range(2):
        flat = 2 * layer + along_x
        plane = flat + core * (3 - 2 * flat)
        for along_y in range(2):
            weight = weight_ref[2 * along_x + along_y]
            for pair in pairs(rows):
                cells = [([layer + along_x, layer + along_x + 1], row + along_y) for row in pair]
                taps = taps_matmul(weight, cells, source, 2)
                for i, row in enumerate(pair):
                    tap = taps[:, i * NZ : (i + 1) * NZ]
                    even = pltpu.roll(tap[48:], 1, 1) + tap[16:32]
                    odd = tap[32:48] + pltpu.roll(tap[:16], NZ - 1, 1)
                    line = pl.ds(2 * row + along_y, 16, stride=32)
                    fine[plane, 0, line, :] = even
                    fine[plane, 1, line, :] = odd


def kernel(
    field_ref, w1_ref, w2_ref, up_ref, out_ref,
    spread, cells, first, second, fine, w1, w2, send, recv,
):
    gx = lax.axis_index("gx")
    gy = lax.axis_index("gy")
    col = lax.axis_index("col")
    core = lax.rem(gx, 2)
    sign = 1 - 2 * core
    partner = {"gx": gx + sign}
    outer = {"gx": lax.rem(gx + 16 - sign, 16)}
    far = {"gx": lax.rem(gx + 16 + 2 * sign, 16)}
    far_back = {"gx": lax.rem(gx + 16 - 2 * sign, 16)}
    up = {"gy": lax.rem(gy + 1, 8)}
    down = {"gy": lax.rem(gy + 7, 8)}
    other = {"col": 1 - col}

    barrier = pltpu.get_barrier_semaphore()
    for device in (partner, outer, far, far_back, up, down, other):
        pl.semaphore_signal(barrier, inc=1, device_id=device, device_id_type=MESH)

    def copy(number, source, target, device):
        return pltpu.make_async_remote_copy(
            src_ref=source,
            dst_ref=target,
            send_sem=send.at[number],
            recv_sem=recv.at[number],
            device_id=device,
            device_id_type=MESH,
        )

    def rows_of(buffer, at, source_layer, source_row, target_layer, target_row, count):
        return (
            buffer.at[source_layer + at, block(source_row + at, count)],
            buffer.at[target_layer + at, block(target_row + at, count)],
        )

    mine = pl.ds(pl.multiple_of(col * 96, 96), 96)

    def same(ref):
        return ref.at[mine], ref.at[mine]

    a = functools.partial(rows_of, cells, 3)
    f = functools.partial(rows_of, first, 2)
    s = functools.partial(rows_of, second, 1)
    both = pl.ds(3, 2)
    copies = [
        copy(0, *same(w1), other),
        copy(1, *same(w2), other),
        copy(2, *a(1, 0, 2, 0, 16), partner),
        copy(3, *a(0, 0, -1, 0, 3), outer),
        copy(4, *a(0, 13, -1, 13, 3), outer),
        copy(5, *a(1, 0, -2, 0, 3), outer),
        copy(6, *a(1, 13, -2, 13, 3), outer),
        copy(7, *a(1, 0, -3, 0, 3), far),
        copy(8, *a(1, 13, -3, 13, 3), far),
        copy(9, *a(0, 3, -1, 3, 10), outer),
        copy(10, *a(1, 3, -2, 3, 10), outer),
        copy(11, *a(1, 3, -3, 3, 10), far),
        copy(12, cells.at[both, block(3, 3)], cells.at[both, block(19, 3)], down),
        copy(13, cells.at[both, block(16, 3)], cells.at[both, block(0, 3)], up),
        copy(14, *a(-1, 0, -1, 16, 3), down),
        copy(15, *a(-1, 13, -1, -3, 3), up),
        copy(16, *a(-2, 0, -2, 16, 3), down),
        copy(17, *a(-2, 13, -2, -3, 3), up),
        copy(18, *a(-3, 0, -3, 16, 3), down),
        copy(19, *a(-3, 13, -3, -3, 3), up),
        copy(20, *a(1, -3, 2, -3, 3), partner),
        copy(21, *a(1, 16, 2, 16, 3), partner),
        copy(22, *f(1, 1, 2, 1, 14), partner),
        copy(23, *f(1, -2, 2, -2, 3), partner),
        copy(24, *f(1, 15, 2, 15, 3), partner),
        copy(25, *s(1, 2, 2, 2, 12), partner),
        copy(26, *s(1, -1, 2, -1, 3), partner),
        copy(27, *s(1, 14, 2, 14, 3), partner),
    ]

    def start(*numbers):
        for number in numbers:
            copies[number].start()

    def arrive(*numbers):
        for number in numbers:
            copies[number].wait_recv()

    def assemble(source, target):
        for along_x in range(3):
            for along_y in range(3):
                piece = source[along_x + core * (2 - 2 * along_x), along_y].reshape(96, C)
                k = 3 * along_x + along_y
                target[mine, k * C : (k + 1) * C] = piece

    def lay_out(rows):
        for layer in range(2):
            plane = layer + core * (1 - 2 * layer)
            for row in rows:
                value = spread[pl.ds(plane * ROWS + row, C, stride=2 * ROWS), :]
                cells[layer + 3, block(row + 3, 1), :] = value.astype(jnp.bfloat16)

    assemble(w1_ref, w1)
    for i in range(8):
        spread[i * 256 : (i + 1) * 256, :] = field_ref[8 * i : 8 * i + 8].astype(jnp.float32).reshape(256, NZ)
    lay_out((0, 1, 2, 13, 14, 15))
    pl.semaphore_wait(barrier, 7)
    start(0, 3, 4, 5, 6, 7, 8, 12, 13)
    lay_out(range(3, 13))
    start(2, 9, 10, 11)
    assemble(w2_ref, w2)
    start(1)

    conv_1 = functools.partial(convolve, w1, cells, 3, first, 2)
    conv_2 = functools.partial(convolve, w2, first, 2, second, 1)
    conv_up = functools.partial(refine, core, up_ref, second, fine)

    arrive(0, 2)
    conv_1(1, MIDDLE)
    arrive(12, 13)
    start(20, 21)
    arrive(3, 4)
    start(14, 15)
    arrive(5, 6)
    start(16, 17)
    arrive(7, 8)
    start(18, 19)
    start(22)
    arrive(9)
    conv_1(0, MIDDLE)
    arrive(20, 21)
    conv_1(1, BORDER)
    arrive(10)
    conv_1(-1, MIDDLE)
    start(23, 24)
    arrive(22, 1)
    conv_2(1, MIDDLE_2)
    conv_2(0, MIDDLE_2)
    start(25)
    arrive(11)
    conv_1(-2, MIDDLE)
    arrive(25)
    conv_up(1, MIDDLE_3)
    conv_2(-1, MIDDLE_2)
    conv_up(0, MIDDLE_3)
    arrive(14, 15)
    conv_1(0, BORDER)
    arrive(23, 24)
    conv_2(1, BORDER_2)
    arrive(16, 17)
    conv_1(-1, BORDER)
    start(26, 27)
    conv_2(0, BORDER_2)
    arrive(18, 19)
    conv_1(-2, BORDER)
    conv_2(-1, BORDER_2)
    arrive(26, 27)
    conv_up(1, BORDER_3)
    conv_up(0, BORDER_3)

    source = lax.broadcasted_iota(jnp.int32, (2 * NZ, 2 * NZ), 0)
    target = lax.broadcasted_iota(jnp.int32, (2 * NZ, 2 * NZ), 1)
    wanted = jnp.where(source < NZ, 2 * source, 2 * source - 2 * NZ + 1)
    interleave = jnp.where(target == wanted, 1.0, 0.0).astype(jnp.bfloat16)
    for plane in range(4):
        for part in range(4):
            lines = pl.ds(part * 128, 128)
            halves = jnp.concatenate([fine[plane, 0, lines, :], fine[plane, 1, lines, :]], axis=1)
            whole = jnp.dot(halves.astype(jnp.bfloat16), interleave, preferred_element_type=jnp.float32)
            out_ref[4 * part : 4 * part + 4, plane] = whole.astype(jnp.bfloat16).reshape(4, 32, 2 * NZ)

    for number in range(COPIES):
        copies[number].wait_send()


def per_device(field, first_weight, second_weight, up_weight):
    core = lax.rem(lax.axis_index("gx"), 2)
    taps = up_weight.transpose(2, 3, 4, 0, 1)
    taps = jnp.where(core == 0, taps, taps[::-1])
    groups = []
    for along_x in range(2):
        for along_y in range(2):
            group = taps[3 - along_x :: -2, 3 - along_y :: -2]
            groups.append(group.transpose(2, 3, 0, 1, 4).reshape(64, 4 * C))
    up = jnp.stack(groups)
    vmem = pl.BlockSpec(memory_space=pltpu.VMEM)
    return pl.pallas_call(
        kernel,
        out_shape=jax.ShapeDtypeStruct((16, 4, 32, 2 * NZ), jnp.bfloat16),
        in_specs=[vmem] * 4,
        out_specs=vmem,
        scratch_shapes=[
            pltpu.VMEM((2 * C * ROWS, NZ), jnp.float32),
            pltpu.VMEM((6, 22 * C, NZ), jnp.bfloat16),
            pltpu.VMEM((5, 20 * C, NZ), jnp.bfloat16),
            pltpu.VMEM((4, 18 * C, NZ), jnp.bfloat16),
            pltpu.VMEM((4, 2, 512, NZ), jnp.float32),
            pltpu.VMEM((192, 9 * C), jnp.bfloat16),
            pltpu.VMEM((192, 9 * C), jnp.bfloat16),
            pltpu.SemaphoreType.DMA((COPIES,)),
            pltpu.SemaphoreType.DMA((COPIES,)),
        ],
        compiler_params=pltpu.CompilerParams(
            collective_id=0, has_side_effects=True, vmem_limit_bytes=48 << 20
        ),
        name="decoder",
    )(
        field,
        first_weight.transpose(2, 3, 4, 0, 1),
        second_weight.transpose(2, 3, 4, 0, 1),
        up,
    )


def solution(mesh):
    in_specs = (
        P(None, "gx", "gy", None),
        P("col", None, None, None, None),
        P("col", None, None, None, None),
        P("col", None, None, None, None),
    )
    out_specs = P("col", "gx", "gy", None)
    return jax.shard_map(per_device, mesh=mesh, in_specs=in_specs, out_specs=out_specs, check_vma=False)
```

profile of v0, /device:TPU:1, one launch (start us, length us, event | category | flops | bytes accessed | tf_op | source)
XLA Modules:
  0.0 34.4 jit_solution(2994176304544035244)
XLA Ops:
  0.0 1.2 %reverse_select_fusion = bf16[4,4,4,16,64]{4,2,1,0,3:T(4,128)(2,1)S(1)} fusion(bf16[4,4,4,16,64]{4,2,1,0,3:T(4,128)(2,1)} %bitcast.13, pred[]{:T(512)S(6)} %eq.3), kind=kLoop, calls=%fused_computation | loop fusion | flops 65536 | bytes 262145 | tf_op jit(solution)/shard_map/jit(_where)/select_n | solution.py:245
  1.2 0.1 fusion
  1.3 0.1 copy.6
  1.4 0.1 stack_reshape.13
  1.5 0.1 copy.5
  1.6 0.0 copy-start
  1.6 0.1 stack_reshape.12
  1.7 0.1 copy.8
  1.8 0.1 stack_reshape.15
  1.9 0.0 copy-start.1
  1.9 0.0 copy-start.2
  1.9 0.1 copy.7
  2.0 0.1 stack_reshape.14
  2.1 0.5 %copy-done = bf16[64,2,16,128]{3,2,1,0:T(8,128)(2,1)S(1)} copy-done((bf16[64,2,16,128]{3,2,1,0:T(8,128)(2,1)S(1)}, bf16[64,2,16,128]{3,2,1,0:T(8,128)(2,1)}, u32[]{:S(2)}) %copy-start) | copy-done | bytes 524312
  2.6 0.3 copy-done.1
  2.9 0.1 copy-done.2
  3.0 30.5 %decoder.1 = bf16[16,4,32,256]{3,2,1,0:T(8,128)(2,1)S(1)} custom-call(bf16[64,2,16,128]{3,2,1,0:T(8,128)(2,1)S(1)} %copy-done, bf16[3,3,3,32,64]{4,3,2,1,0:T(8,128)(2,1)S(1)} %bitcast.11, bf16[3,3,3,32,64]{4,3,2,1,0:T(8,128)(2,1)S(1)} %bitcast.12, bf16[4,64,256]{2,1,0:T(8,128)(2,1)S(1)} %pad_maximum_fusion.up_ref), custom_call_target="tpu_custom_call" | custom-call | tf_op jit(solution)/shard_map/decoder/pallas_call | solution.py:253
  33.4 1.0 %copy.10 = bf16[16,4,32,256]{3,2,1,0:T(8,128)(2,1)} copy(bf16[16,4,32,256]{3,2,1,0:T(8,128)(2,1)S(1)} %decoder.1) | data formatting | bytes 2097152
  (3 shorter events, 0.1 us)
Async XLA Ops:
  1.6 1.0 %copy-start = (bf16[64,2,16,128]{3,2,1,0:T(8,128)(2,1)S(1)}, bf16[64,2,16,128]{3,2,1,0:T(8,128)(2,1)}, u32[]{:S(2)}) copy-start(bf16[64,2,16,128]{3,2,1,0:T(8,128)(2,1)} %field_ref.1) | copy-start | bytes 1572868
  1.9 1.0 %copy-start.1 = (bf16[32,64,3,3,3]{1,0,4,3,2:T(8,128)(2,1)S(1)}, bf16[32,64,3,3,3]{1,0,4,3,2:T(8,128)(2,1)}, u32[]{:S(2)}) copy-start(bf16[32,64,3,3,3]{1,0,4,3,2:T(8,128)(2,1)} %param.5) | copy-start | bytes 331780
  1.9 1.0 %copy-start.2 = (bf16[32,64,3,3,3]{1,0,4,3,2:T(8,128)(2,1)S(1)}, bf16[32,64,3,3,3]{1,0,4,3,2:T(8,128)(2,1)}, u32[]{:S(2)}) copy-start(bf16[32,64,3,3,3]{1,0,4,3,2:T(8,128)(2,1)} %param.6) | copy-start | bytes 331780
where the time goes:
time: 34.5 us; the launch traced here: 34.4 us
  Pallas kernels  30.5 us (88%)
  local copies, waits for them, and re-layouts  2.65 us (8%)
  other arithmetic  1.19 us (3%)
    pallas_call x1, Pallas kernels, per_device(): pl.pallas_call(kernel, out_shape=jax.ShapeDtypeStruct((16, 4, 32, 2 * NZ)...  30.5 us
    unnamed x7, local copies, waits for them, and re-layouts  1.81 us
    select_n x1, other arithmetic, per_device(): taps = jnp.where(core == 0, taps, taps[::-1])  1.17 us

commit v1 on v0

--- a/solution.py
+++ b/solution.py
@@ -68,8 +68,9 @@
 
 
 def kernel(
+    field_in, w1_in, w2_in, up_in, out,
     field_ref, w1_ref, w2_ref, up_ref, out_ref,
-    spread, cells, first, second, fine, w1, w2, send, recv,
+    spread, cells, first, second, fine, w1, w2, up_taps, up_weight, send, recv, load, store,
 ):
     gx = lax.axis_index("gx")
     gy = lax.axis_index("gy")
@@ -87,6 +88,15 @@
     barrier = pltpu.get_barrier_semaphore()
     for device in (partner, outer, far, far_back, up, down, other):
         pl.semaphore_signal(barrier, inc=1, device_id=device, device_id_type=MESH)
+
+    loads = [
+        pltpu.make_async_copy(source, target, load.at[i])
+        for i, (source, target) in enumerate(
+            ((field_in, field_ref), (w1_in, w1_ref), (w2_in, w2_ref), (up_in, up_ref))
+        )
+    ]
+    for local in loads:
+        local.start()
 
     def copy(number, source, target, device):
         return pltpu.make_async_remote_copy(
@@ -159,6 +169,21 @@
                 k = 3 * along_x + along_y
                 target[mine, k * C : (k + 1) * C] = piece
 
+    def assemble_up():
+        for along_x in range(4):
+            for o in range(16):
+                piece = up_ref[o, along_x + core * (3 - 2 * along_x)].astype(jnp.float32)
+                for along_y in range(4):
+                    up_taps[4 * along_x + along_y, 4 * o : 4 * o + 4, :] = piece[along_y]
+        for x in range(4):
+            for y in range(4):
+                k = 2 * (1 - x // 2) + 1 - y // 2
+                for z in range(4):
+                    value = up_taps[4 * x + y, pl.ds(z, 16, stride=4), :]
+                    up_weight[2 * ((3 - x) % 2) + (3 - y) % 2, 16 * z : 16 * z + 16, k * C : (k + 1) * C] = (
+                        value.astype(jnp.bfloat16)
+                    )
+
     def lay_out(rows):
         for layer in range(2):
             plane = layer + core * (1 - 2 * layer)
@@ -166,7 +191,9 @@
                 value = spread[pl.ds(plane * ROWS + row, C, stride=2 * ROWS), :]
                 cells[layer + 3, block(row + 3, 1), :] = value.astype(jnp.bfloat16)
 
+    loads[1].wait()
     assemble(w1_ref, w1)
+    loads[0].wait()
     for i in range(8):
         spread[i * 256 : (i + 1) * 256, :] = field_ref[8 * i : 8 * i + 8].astype(jnp.float32).reshape(256, NZ)
     lay_out((0, 1, 2, 13, 14, 15))
@@ -174,12 +201,15 @@
     start(0, 3, 4, 5, 6, 7, 8, 12, 13)
     lay_out(range(3, 13))
     start(2, 9, 10, 11)
+    loads[2].wait()
     assemble(w2_ref, w2)
     start(1)
+    loads[3].wait()
+    assemble_up()
 
     conv_1 = functools.partial(convolve, w1, cells, 3, first, 2)
     conv_2 = functools.partial(convolve, w2, first, 2, second, 1)
-    conv_up = functools.partial(refine, core, up_ref, second, fine)
+    conv_up = functools.partial(refine, core, up_weight, second, fine)
 
     arrive(0, 2)
     conv_1(1, MIDDLE)
@@ -228,34 +258,35 @@
     target = lax.broadcasted_iota(jnp.int32, (2 * NZ, 2 * NZ), 1)
     wanted = jnp.where(source < NZ, 2 * source, 2 * source - 2 * NZ + 1)
     interleave = jnp.where(target == wanted, 1.0, 0.0).astype(jnp.bfloat16)
+    stores = []
     for plane in range(4):
         for part in range(4):
             lines = pl.ds(part * 128, 128)
             halves = jnp.concatenate([fine[plane, 0, lines, :], fine[plane, 1, lines, :]], axis=1)
             whole = jnp.dot(halves.astype(jnp.bfloat16), interleave, preferred_element_type=jnp.float32)
             out_ref[4 * part : 4 * part + 4, plane] = whole.astype(jnp.bfloat16).reshape(4, 32, 2 * NZ)
+        stores.append(pltpu.make_async_copy(out_ref.at[:, plane], out.at[:, plane], store.at[plane]))
+        stores[plane].start()
 
     for number in range(COPIES):
         copies[number].wait_send()
+    for local in stores:
+        local.wait()
 
 
 def per_device(field, first_weight, second_weight, up_weight):
-    core = lax.rem(lax.axis_index("gx"), 2)
-    taps = up_weight.transpose(2, 3, 4, 0, 1)
-    taps = jnp.where(core == 0, taps, taps[::-1])
-    groups = []
-    for along_x in range(2):
-        for along_y in range(2):
-            group = taps[3 - along_x :: -2, 3 - along_y :: -2]
-            groups.append(group.transpose(2, 3, 0, 1, 4).reshape(64, 4 * C))
-    up = jnp.stack(groups)
-    vmem = pl.BlockSpec(memory_space=pltpu.VMEM)
+    hbm = pl.BlockSpec(memory_space=pltpu.HBM)
     return pl.pallas_call(
         kernel,
-        out_shape=jax.ShapeDtypeStruct((16, 4, 32, 2 * NZ), jnp.bfloat16),
-        in_specs=[vmem] * 4,
-        out_specs=vmem,
+        out_shape=pltpu.HBM((16, 4, 32, 2 * NZ), jnp.bfloat16),
+        in_specs=[hbm] * 4,
+        out_specs=hbm,
         scratch_shapes=[
+            pltpu.VMEM((C, 2, ROWS, NZ), jnp.bfloat16),
+            pltpu.VMEM((3, 3, 3, 32, C), jnp.bfloat16),
+            pltpu.VMEM((3, 3, 3, 32, C), jnp.bfloat16),
+            pltpu.VMEM((16, 4, 4, 4, C), jnp.bfloat16),
+            pltpu.VMEM((16, 4, 32, 2 * NZ), jnp.bfloat16),
             pltpu.VMEM((2 * C * ROWS, NZ), jnp.float32),
             pltpu.VMEM((6, 22 * C, NZ), jnp.bfloat16),
             pltpu.VMEM((5, 20 * C, NZ), jnp.bfloat16),
@@ -263,18 +294,27 @@
             pltpu.VMEM((4, 2, 512, NZ), jnp.float32),
             pltpu.VMEM((192, 9 * C), jnp.bfloat16),
             pltpu.VMEM((192, 9 * C), jnp.bfloat16),
+            pltpu.VMEM((16, C, C), jnp.float32),
+            pltpu.VMEM((4, C, 4 * C), jnp.bfloat16),
             pltpu.SemaphoreType.DMA((COPIES,)),
             pltpu.SemaphoreType.DMA((COPIES,)),
+            pltpu.SemaphoreType.DMA((4,)),
+            pltpu.SemaphoreType.DMA((4,)),
         ],
         compiler_params=pltpu.CompilerParams(
             collective_id=0, has_side_effects=True, vmem_limit_bytes=48 << 20
         ),
         name="decoder",
     )(
-        field,
-        first_weight.transpose(2, 3, 4, 0, 1),
-        second_weight.transpose(2, 3, 4, 0, 1),
-        up,
+        *(
+            pltpu.with_memory_space_constraint(value, pltpu.HBM)
+            for value in (
+                field,
+                first_weight.transpose(2, 3, 4, 0, 1),
+                second_weight.transpose(2, 3, 4, 0, 1),
+                up_weight.transpose(0, 2, 3, 4, 1),
+            )
+        )
     )
 
 

time: 34.5 us -> 33.8 us (0.980)
  other arithmetic: 1.19 us -> 0 us
  Pallas kernels: 30.5 us -> 31.3 us
  local copies, waits for them, and re-layouts: 2.65 us -> 2.29 us
    select_n x1 -> x0, other arithmetic: 1.17 us -> none  [per_device(): taps = jnp.where(core == 0, taps, taps[::-1])]
    pallas_call x1, Pallas kernels: 30.5 us -> 31.3 us  [per_device(): pl.pallas_call(kernel, out_shape=pltpu.HBM((16, 4, 32, 2 * NZ), jnp.bfloa...]
    unnamed x7 -> x1, local copies, waits for them, and re-layouts: 1.81 us -> 2.29 us
    another operation x4 -> x0, local copies, waits for them, and re-layouts: 0.45 us -> none  [per_device(): up = jnp.stack(groups)]
where the time goes in v1:
time: 33.8 us; the launch traced here: 33.6 us
  Pallas kernels  31.3 us (93%)
  local copies, waits for them, and re-layouts  2.29 us (7%)
    pallas_call x1, Pallas kernels, per_device(): pl.pallas_call(kernel, out_shape=pltpu.HBM((16, 4, 32, 2 * NZ), jnp.bfloa...  31.3 us
    unnamed x1, local copies, waits for them, and re-layouts  2.29 us

profile of v1, /device:TPU:1, one launch (start us, length us, event | category | flops | bytes accessed | tf_op | source)
XLA Modules:
  0.0 33.6 jit_solution(13319097146261775678)
XLA Ops:
  0.0 31.3 %decoder.1 = bf16[16,4,32,256]{3,2,1,0:T(8,128)(2,1)} custom-call(bf16[64,2,16,128]{3,2,1,0:T(8,128)(2,1)} %field_in.1, bf16[3,3,3,32,64]{4,3,2,1,0:T(8,128)(2,1)} %bitcast.4, bf16[3,3,3,32,64]{4,3,2,1,0:T(8,128)(2,1)} %bitcast.5, bf16[16,4,4,4,64]{4,3,2,1,0:T(4,128)(2,1)} %bitcast.3), custom_call_target="tpu_custom_call" | custom-call | tf_op jit(solution)/shard_map/decoder/pallas_call | solution.py:279
  31.4 2.3 %copy.6 = bf16[16,4,32,256]{3,2,1,0:T(8,128)(2,1)} copy(bf16[16,4,32,256]{3,2,1,0:T(8,128)(2,1)} %decoder.1) | data formatting | bytes 2097152

commit v2 on v1

--- a/solution.py
+++ b/solution.py
@@ -68,9 +68,9 @@
 
 
 def kernel(
-    field_in, w1_in, w2_in, up_in, out,
-    field_ref, w1_ref, w2_ref, up_ref, out_ref,
-    spread, cells, first, second, fine, w1, w2, up_taps, up_weight, send, recv, load, store,
+    field_in, w1_in, w2_in, up_in, out_ref,
+    field_ref, w1_ref, w2_ref, up_ref,
+    spread, cells, first, second, fine, w1, w2, up_taps, up_weight, send, recv, load,
 ):
     gx = lax.axis_index("gx")
     gy = lax.axis_index("gy")
@@ -205,14 +205,28 @@
     assemble(w2_ref, w2)
     start(1)
     loads[3].wait()
-    assemble_up()
 
     conv_1 = functools.partial(convolve, w1, cells, 3, first, 2)
     conv_2 = functools.partial(convolve, w2, first, 2, second, 1)
     conv_up = functools.partial(refine, core, up_weight, second, fine)
 
+    source = lax.broadcasted_iota(jnp.int32, (2 * NZ, 2 * NZ), 0)
+    target = lax.broadcasted_iota(jnp.int32, (2 * NZ, 2 * NZ), 1)
+    wanted = jnp.where(source < NZ, 2 * source, 2 * source - 2 * NZ + 1)
+    interleave = jnp.where(target == wanted, 1.0, 0.0).astype(jnp.bfloat16)
+
+    def weave(layer):
+        for flat in (2 * layer, 2 * layer + 1):
+            plane = flat + core * (3 - 2 * flat)
+            for part in range(4):
+                lines = pl.ds(part * 128, 128)
+                halves = jnp.concatenate([fine[plane, 0, lines, :], fine[plane, 1, lines, :]], axis=1)
+                whole = jnp.dot(halves.astype(jnp.bfloat16), interleave, preferred_element_type=jnp.float32)
+                out_ref[4 * part : 4 * part + 4, plane] = whole.astype(jnp.bfloat16).reshape(4, 32, 2 * NZ)
+
     arrive(0, 2)
     conv_1(1, MIDDLE)
+    start(22)
     arrive(12, 13)
     start(20, 21)
     arrive(3, 4)
@@ -221,72 +235,57 @@
     start(16, 17)
     arrive(7, 8)
     start(18, 19)
-    start(22)
+    assemble_up()
+    arrive(20, 21)
+    conv_1(1, BORDER)
+    start(23, 24)
     arrive(9)
     conv_1(0, MIDDLE)
-    arrive(20, 21)
-    conv_1(1, BORDER)
-    arrive(10)
-    conv_1(-1, MIDDLE)
-    start(23, 24)
     arrive(22, 1)
     conv_2(1, MIDDLE_2)
-    conv_2(0, MIDDLE_2)
     start(25)
-    arrive(11)
-    conv_1(-2, MIDDLE)
-    arrive(25)
-    conv_up(1, MIDDLE_3)
-    conv_2(-1, MIDDLE_2)
-    conv_up(0, MIDDLE_3)
     arrive(14, 15)
     conv_1(0, BORDER)
     arrive(23, 24)
     conv_2(1, BORDER_2)
+    start(26, 27)
+    arrive(10)
+    conv_1(-1, MIDDLE)
+    conv_2(0, MIDDLE_2)
+    arrive(25)
+    conv_up(1, MIDDLE_3)
     arrive(16, 17)
     conv_1(-1, BORDER)
-    start(26, 27)
     conv_2(0, BORDER_2)
+    arrive(26, 27)
+    conv_up(1, BORDER_3)
+    weave(1)
+    arrive(11)
+    conv_1(-2, MIDDLE)
     arrive(18, 19)
     conv_1(-2, BORDER)
+    conv_2(-1, MIDDLE_2)
     conv_2(-1, BORDER_2)
-    arrive(26, 27)
-    conv_up(1, BORDER_3)
+    conv_up(0, MIDDLE_3)
     conv_up(0, BORDER_3)
-
-    source = lax.broadcasted_iota(jnp.int32, (2 * NZ, 2 * NZ), 0)
-    target = lax.broadcasted_iota(jnp.int32, (2 * NZ, 2 * NZ), 1)
-    wanted = jnp.where(source < NZ, 2 * source, 2 * source - 2 * NZ + 1)
-    interleave = jnp.where(target == wanted, 1.0, 0.0).astype(jnp.bfloat16)
-    stores = []
-    for plane in range(4):
-        for part in range(4):
-            lines = pl.ds(part * 128, 128)
-            halves = jnp.concatenate([fine[plane, 0, lines, :], fine[plane, 1, lines, :]], axis=1)
-            whole = jnp.dot(halves.astype(jnp.bfloat16), interleave, preferred_element_type=jnp.float32)
-            out_ref[4 * part : 4 * part + 4, plane] = whole.astype(jnp.bfloat16).reshape(4, 32, 2 * NZ)
-        stores.append(pltpu.make_async_copy(out_ref.at[:, plane], out.at[:, plane], store.at[plane]))
-        stores[plane].start()
+    weave(0)
 
     for number in range(COPIES):
         copies[number].wait_send()
-    for local in stores:
-        local.wait()
 
 
 def per_device(field, first_weight, second_weight, up_weight):
     hbm = pl.BlockSpec(memory_space=pltpu.HBM)
     return pl.pallas_call(
         kernel,
-        out_shape=pltpu.HBM((16, 4, 32, 2 * NZ), jnp.bfloat16),
+        out_shape=jax.ShapeDtypeStruct((16, 4, 32, 2 * NZ), jnp.bfloat16),
         in_specs=[hbm] * 4,
-        out_specs=hbm,
+        out_specs=pl.BlockSpec(memory_space=pltpu.VMEM),
         scratch_shapes=[
             pltpu.VMEM((C, 2, ROWS, NZ), jnp.bfloat16),
             pltpu.VMEM((3, 3, 3, 32, C), jnp.bfloat16),
             pltpu.VMEM((3, 3, 3, 32, C), jnp.bfloat16),
             pltpu.VMEM((16, 4, 4, 4, C), jnp.bfloat16),
-            pltpu.VMEM((16, 4, 32, 2 * NZ), jnp.bfloat16),
             pltpu.VMEM((2 * C * ROWS, NZ), jnp.float32),
             pltpu.VMEM((6, 22 * C, NZ), jnp.bfloat16),
             pltpu.VMEM((5, 20 * C, NZ), jnp.bfloat16),
@@ -298,7 +297,6 @@
             pltpu.VMEM((4, C, 4 * C), jnp.bfloat16),
             pltpu.SemaphoreType.DMA((COPIES,)),
             pltpu.SemaphoreType.DMA((COPIES,)),
-            pltpu.SemaphoreType.DMA((4,)),
             pltpu.SemaphoreType.DMA((4,)),
         ],
         compiler_params=pltpu.CompilerParams(

time: 33.8 us -> 31 us (0.917)
  Pallas kernels: 31.3 us -> 29.9 us
  local copies, waits for them, and re-layouts: 2.29 us -> 0.97 us
    pallas_call x1, Pallas kernels: 31.3 us -> 29.9 us  [per_device(): pl.pallas_call(kernel, out_shape=jax.ShapeDtypeStruct((16, 4, 32, 2 * NZ)...]
    unnamed x1, local copies, waits for them, and re-layouts: 2.29 us -> 0.97 us
where the time goes in v2:
time: 31 us; the launch traced here: 30.9 us
  Pallas kernels  29.9 us (96%)
  local copies, waits for them, and re-layouts  0.97 us (3%)
    pallas_call x1, Pallas kernels, per_device(): pl.pallas_call(kernel, out_shape=jax.ShapeDtypeStruct((16, 4, 32, 2 * NZ)...  29.9 us
    unnamed x1, local copies, waits for them, and re-layouts  0.97 us

profile of v2, /device:TPU:1, one launch (start us, length us, event | category | flops | bytes accessed | tf_op | source)
XLA Modules:
  0.0 30.9 jit_solution(10375910351786185809)
XLA Ops:
  0.0 29.9 %decoder.1 = bf16[16,4,32,256]{3,2,1,0:T(8,128)(2,1)S(1)} custom-call(bf16[64,2,16,128]{3,2,1,0:T(8,128)(2,1)} %field_in.1, bf16[3,3,3,32,64]{4,3,2,1,0:T(8,128)(2,1)} %bitcast.4, bf16[3,3,3,32,64]{4,3,2,1,0:T(8,128)(2,1)} %bitcast.5, bf16[16,4,4,4,64]{4,3,2,1,0:T(4,128)(2,1)} %bitcast.3), custom_call_target="tpu_custom_call" | custom-call | tf_op jit(solution)/shard_map/decoder/pallas_call | solution.py:279
  29.9 1.0 %copy.6 = bf16[16,4,32,256]{3,2,1,0:T(8,128)(2,1)} copy(bf16[16,4,32,256]{3,2,1,0:T(8,128)(2,1)S(1)} %decoder.1) | data formatting | bytes 2097152
